TPU v7x, 128 devices: a whole 4x4x4 slice. The times are simulated.
128 devices in a mesh: row: 16 (over z_lo, y, core), col: 8 (over x, z_hi).
Axes of the slice: x: 4, y: 4, z: 4 (z_hi: 2, z_lo: 2; z = z_hi * 2 + z_lo), core: 2. Of those that a mesh axis runs over, the one named last changes fastest.
Arguments:
- queries: bfloat16 [8, 128, 4096], P(None, 'row', 'col'), may hold values from -13 to 13, as said below
- key_cache: bfloat16 [8, 65536, 1024], P(None, ('row', 'col')), may hold values from -13 to 13
- value_cache: bfloat16 [8, 65536, 1024], P(None, ('row', 'col')), may hold values from -6 to 6
- key_table: bfloat16 [1024, 1024], replicated, may hold values from -24 to 24
- value_table: bfloat16 [1024, 1024], replicated, may hold values from -6 to 6
- lengths: int32 [8], replicated, may hold values from 8192 to 65536
- token_ids: int32 [8, 128], P(None, 'row'), may hold values from 0 to 1023
Outputs:
- attended: bfloat16 [8, 128, 4096], P(None, 'row', 'col')
Inputs may be any that keep to these rules, and one draw needn't show every extreme that they name: `queries`: entries of the query array lie in the stated range.
All inputs are finite; a program needn't handle non-finite values.
Results may differ from a plain program's by a relative error of at most 0.006.
Values may be sent and summed in bfloat16 or wider, within the bound.
No kernel may reach another device: no remote copies, remote signals or barrier semaphores. Data moves between devices by JAX's collectives and lax.ppermute only.
A program may use at most 192 MiB of HBM per device.

v0:
```python
import jax
import jax.numpy as jnp
from jax import lax
from jax.sharding import PartitionSpec as P

HQ = 32
KH = 8
HD = 128


def laid_out(tiles, dim):
    lengths = list(tiles.shape[1:])
    lengths[dim] *= tiles.shape[0]
    return jnp.moveaxis(tiles, 0, dim).reshape(lengths)


def copy_for_each(array, axis):
    count = lax.axis_size(axis)
    return lax.all_to_all(
        jnp.broadcast_to(array[None], (count, *array.shape)), axis, 0, 0, tiled=True
    )


def gathered_copies(array, axis, dim):
    return laid_out(copy_for_each(array, axis), dim)


def cache_partials(whole, key_cache, value_cache, lengths, offset):
    users, beams, width = whole.shape
    positions = key_cache.shape[1]
    group = HQ // KH
    scale = HD ** (-0.5)

    def one_user(items):
        q_user, k_user, v_user, limit = items
        q_heads = q_user.reshape(beams, KH, group, HD)
        k_heads = k_user.reshape(positions, KH, HD)
        v_heads = v_user.reshape(positions, KH, HD)
        s = (
            jnp.einsum("wkgd,lkd->kwgl", q_heads, k_heads, preferred_element_type=jnp.float32)
            * scale
        )
        live = offset + jnp.arange(positions, dtype=jnp.int32) < limit
        s = jnp.where(live, s, -1e30)
        peak = jnp.max(s, axis=-1)
        weight = jnp.where(live, jnp.exp(s - peak[..., None]), 0.0)
        total = jnp.sum(weight, axis=-1)
        numer = jnp.einsum(
            "kwgl,lkd->wkgd",
            weight.astype(jnp.bfloat16),
            v_heads,
            preferred_element_type=jnp.float32,
        )
        peak = jnp.transpose(peak, (1, 0, 2)).reshape(beams, HQ)
        total = jnp.transpose(total, (1, 0, 2)).reshape(beams, HQ)
        return (numer.reshape(beams, width), peak, total)

    return lax.map(one_user, (whole, key_cache, value_cache, lengths))


def body(queries, key_cache, value_cache, key_table, value_table, lengths, token_ids):
    users, beam_part, width_part = queries.shape
    heads_part = width_part // HD
    scale = HD ** (-0.5)
    row_at = lax.axis_index("row")
    col_at = lax.axis_index("col")
    whole = gathered_copies(queries, "col", 2)
    whole = lax.all_gather(whole, "row", axis=1, tiled=True)
    offset = (row_at * lax.axis_size("col") + col_at) * key_cache.shape[1]
    numer_part, peak_part, total_part = cache_partials(
        whole, key_cache, value_cache, lengths, offset
    )
    peak_all = lax.pmax(peak_part, ("row", "col"))
    factor = jnp.exp(peak_part - peak_all)
    weighted = (numer_part.reshape(users, -1, HQ, HD) * factor[..., None]).reshape(
        users, -1, HQ * HD
    )
    mass = total_part * factor

    def local_part(array, per_head):
        picked = lax.dynamic_slice_in_dim(array, row_at * beam_part, beam_part, 1)
        return lax.dynamic_slice_in_dim(
            picked, col_at * heads_part * per_head, heads_part * per_head, 2
        )

    numer, total = lax.psum((weighted, mass), ("row", "col"))
    numer = local_part(numer, HD)
    total = local_part(total, 1)
    peak = local_part(peak_all, 1)
    codes = jnp.arange(key_table.shape[0], dtype=jnp.int32)
    onehot = (token_ids[..., None] == codes).astype(jnp.bfloat16)
    own_keys = jnp.einsum("uwv,vc->uwc", onehot, key_table, preferred_element_type=jnp.float32)
    own_values = jnp.einsum("uwv,vc->uwc", onehot, value_table, preferred_element_type=jnp.float32)
    group = HQ // KH
    own_keys = jnp.repeat(own_keys.reshape(users, beam_part, KH, HD), group, axis=2)
    own_values = jnp.repeat(own_values.reshape(users, beam_part, KH, HD), group, axis=2)
    own_keys = lax.dynamic_slice_in_dim(own_keys, col_at * heads_part, heads_part, 2)
    own_values = lax.dynamic_slice_in_dim(own_values, col_at * heads_part, heads_part, 2)
    q_local = queries.astype(jnp.float32).reshape(users, beam_part, heads_part, HD)
    own_score = jnp.sum(q_local * own_keys, axis=-1) * scale
    final_peak = jnp.maximum(peak, own_score)
    carried = jnp.exp(peak - final_peak)
    fresh = jnp.exp(own_score - final_peak)
    numer = (
        numer.reshape(users, beam_part, heads_part, HD) * carried[..., None]
        + fresh[..., None] * own_values
    )
    total = total * carried + fresh
    result = numer / total[..., None]
    return result.reshape(users, beam_part, width_part).astype(jnp.bfloat16)


def solution(mesh):
    return jax.shard_map(
        body,
        mesh=mesh,
        in_specs=(
            P(None, "row", "col"),
            P(None, ("row", "col"), None),
            P(None, ("row", "col"), None),
            P(),
            P(),
            P(),
            P(None, "row"),
        ),
        out_specs=P(None, "row", "col"),
        check_vma=False,
    )
```

profile of v0, /device:TPU:1, one launch (start us, length us, event | category | flops | bytes accessed | tf_op | source)
XLA Modules:
  0.0 743.7 jit_solution(7798961752427165654)
XLA Ops:
  7.6 17.5 %all_to_all.5 = bf16[8,8,8,512]{3,2,1,0:T(8,128)(2,1)S(1)} all-to-all(bf16[8,8,8,512]{3,2,1,0:T(8,128)(2,1)S(1)} %broadcast_in_dim.46), channel_id=1, replica_groups=mesh['row'=16,'col'=8] {'col'}, dimensions={0} | all-to-all | bytes 1048576 | tf_op jit(solution)/shard_map/all_to_all | solution.py:19
  26.6 52.4 %all-gather.2.cloned.1.call-done = bf16[8,128,4096]{2,0,1:T(8,128)(2,1)} async-done(((bf16[8,8,4096]{2,0,1:T(8,128)(2,1)}), bf16[8,128,4096]{2,0,1:T(8,128)(2,1)}) %all-gather.2.cloned.1.call-update) | async-done | bytes 8388624 | tf_op jit(solution)/shard_map/all_gather | solution.py:68
  79.0 12.5 %copy.35 = bf16[8,128,4096]{1,2,0:T(8,128)(2,1)} copy(bf16[8,128,4096]{2,0,1:T(8,128)(2,1)} %all-gather.2.cloned.1.call-done) | data formatting | bytes 16777216 | tf_op jit(solution)/shard_map/while | solution.py:58
  91.5 240.9 %while.14 = (s32[]{:T(128)}, f32[8,128,4096]{2,1,0:T(8,128)}, f32[8,128,32]{1,2,0:T(8,128)}, f32[8,128,32]{1,2,0:T(8,128)S(1)}, bf16[8,512,1024]{2,1,0:T(8,128)(...) while((s32[]{:T(128)}, f32[8,128,4096]{2,1,0:T(8,128)}, ...), condition=%wide.region_3.4_spmd, body=%wide.region_0.3_spmd.sunk | while | flops 1100997632 | bytes 82971808 | solution.py:58
  96.7 2.8 fusion.45
  99.6 3.2 copy-done.1
  108.4 7.2 fusion.46
  115.6 2.9 copy.56
  118.5 3.1 constant_dynamic-update-slice_fusion.2
  126.8 2.8 fusion.45
  129.7 3.2 copy-done.1
  138.5 7.2 fusion.46
  145.7 2.9 copy.56
  148.6 3.1 constant_dynamic-update-slice_fusion.2
  156.9 2.8 fusion.45
  159.8 3.2 copy-done.1
  168.6 7.2 fusion.46
  175.8 2.9 copy.56
  178.7 3.1 constant_dynamic-update-slice_fusion.2
  187.0 2.8 fusion.45
  189.9 3.2 copy-done.1
  198.7 7.2 fusion.46
  205.9 2.9 copy.56
  208.8 3.1 constant_dynamic-update-slice_fusion.2
  217.1 2.8 fusion.45
  220.0 3.2 copy-done.1
  228.8 7.2 fusion.46
  236.0 2.9 copy.56
  238.9 3.1 constant_dynamic-update-slice_fusion.2
  250.1 3.2 copy-done.1
  258.9 7.2 fusion.46
  266.1 2.9 copy.56
  269.0 3.1 constant_dynamic-update-slice_fusion.2
  277.4 2.8 fusion.45
  280.3 3.2 copy-done.1
  289.0 7.2 fusion.46
  296.2 2.9 copy.56
  299.1 3.1 constant_dynamic-update-slice_fusion.2
  307.5 2.8 fusion.45
  310.4 3.2 copy-done.1
  319.2 7.2 fusion.46
  326.4 2.9 copy.56
  329.3 3.1 constant_dynamic-update-slice_fusion.2
  332.5 140.7 %all-reduce.4.cloned.1.call-done = f32[8,128,32]{1,2,0:T(8,128)} async-done(((f32[8,128,32]{1,2,0:T(8,128)}), f32[8,128,32]{1,2,0:T(8,128)}) %all-reduce.4.cloned.1.call-update) | async-done | bytes 131088 | tf_op jit(solution)/shard_map/pmax | solution.py:73
  475.0 8.4 %mul.66 = f32[8,128,32,128]{3,2,1,0:T(8,128)} broadcast(f32[8,128,32]{2,1,0:T(8,128)S(1)} %copy.37), dimensions={0,1,2} | broadcast | bytes 16908288 | tf_op jit(solution)/shard_map/mul | solution.py:75
  483.4 18.2 %mul.67 = f32[8,128,4096]{2,1,0:T(8,128)} reshape(f32[8,128,32,128]{3,2,1,0:T(8,128)} %mul.66) | data formatting | bytes 33554432 | tf_op jit(solution)/shard_map/mul | solution.py:75
  501.6 17.8 %mul.68 = f32[8,128,4096]{2,1,0:T(8,128)} multiply(f32[8,128,4096]{2,1,0:T(8,128)} %get-tuple-element.54, f32[8,128,4096]{2,1,0:T(8,128)} %mul.67) | non-fusion elementwise | flops 4194304 | bytes 50331648 | tf_op jit(solution)/shard_map/mul | solution.py:75
  523.0 211.3 %all-reduce.6.cloned.1.call-done = (f32[8,128,32]{1,2,0:T(8,128)}, f32[8,128,4096]{2,1,0:T(8,128)}) async-done(((f32[8,128,32]{1,2,0:T(8,128)}, f32[8,128,4096]{2,1,0:T(8,128)}), (f32[8,128,32]{1,2,0:T(8,128)}, f32[8,128,4096]{2,1,0:T(8,128)})) %all-reduce.6.cloned.1.call-update) | async-done | bytes 16908304 | tf_op jit(solution)/shard_map/psum | solution.py:86
  (110 shorter events, 99.8 us)
Async XLA Ops:
  6.5 512.9 %copy-start = (bf16[1024,1024]{1,0:T(8,128)(2,1)S(1)}, bf16[1024,1024]{1,0:T(8,128)(2,1)}, u32[]{:S(2)}) copy-start(bf16[1024,1024]{1,0:T(8,128)(2,1)} %param.12) | copy-start | bytes 6291460
  6.5 72.5 %all-gather.2.cloned.1.call-start = ((), (), s32[]{:S(2)}) async-start(), calls=%async_computation.1 | async-start | bytes 8912896 | tf_op jit(solution)/shard_map/all_gather | solution.py:68
  26.5 446.7 %all-reduce.4.cloned.1.call-start = ((), (), s32[]{:S(2)}) async-start(), calls=%async_computation.2 | async-start | bytes 262144 | tf_op jit(solution)/shard_map/pmax | solution.py:73
  26.6 64.9 %copy-start.4 = (s32[8]{0:T(128)S(1)}, s32[8]{0:T(128)}, u32[]{:S(2)}) copy-start(s32[8]{0:T(128)} %param.14) | copy-start | bytes 100
  99.6 3.2 copy-start.1
  129.7 3.2 copy-start.1
  159.8 3.2 copy-start.1
  189.9 3.2 copy-start.1
  220.0 3.2 copy-start.1
  250.1 3.2 copy-start.1
  280.2 3.2 copy-start.1
  310.4 3.2 copy-start.1
  332.4 401.9 %all-reduce.6.cloned.1.call-start = ((), (), s32[]{:S(2)}) async-start(), calls=%async_computation.3 | async-start | bytes 33816576 | tf_op jit(solution)/shard_map/psum | solution.py:86
  519.4 0.7 copy-start.3
  519.4 1.3 copy-start.2
Sparse Core Ops, SparseCore 0:
  26.6 52.3 all-gather.1
  332.5 140.5 all-reduce.3
  519.6 214.6 all-reduce.5
where the time goes:
time: 747 us; the launch traced here: 744 us
  waiting for transfers between devices  404 us (54%)
  local copies, waits for them, and re-layouts  179 us (24%)
  matrix products  82.9 us (11%)
  other arithmetic  46.2 us (6%)
  blocking collectives  17.5 us (2%)
  between operations  13.2 us (2%)
    psum x1, waiting for transfers between devices, body(): numer, total = lax.psum((weighted, mass), ('row', 'col'))  211 us
    pmax x1, waiting for transfers between devices, body(): peak_all = lax.pmax(peak_part, ('row', 'col'))  141 us
    dynamic_slice x48, local copies, waits for them, and re-layouts, cache_partials(): return lax.map(one_user, (whole, key_cache, value_cache, lengths))  57.7 us
    dot_general x8, matrix products, one_user(): jnp.einsum('kwgl,lkd->wkgd', weight.astype(jnp.bfloat16), v_heads, prefer...  57.5 us
    dynamic_update_slice x24, local copies, waits for them, and re-layouts, cache_partials(): return lax.map(one_user, (whole, key_cache, value_cache, lengths))  53.1 us
    all_gather x1, waiting for transfers between devices, body(): whole = lax.all_gather(whole, 'row', axis=1, tiled=True)  52.4 us
    mul x2, local copies, waits for them, and re-layouts, body(): numer_part.reshape(users, -1, HQ, HD) * factor[..., None]  26.6 us
    while x16, local copies, waits for them, and re-layouts  25.8 us
  transfers between devices with their start and end apart: 3, of which 3 were waited for; matrix products, arithmetic and copies ran while one was open for 0% of the time, Pallas kernels for 0%

commit v1 on v0

--- a/solution.py
+++ b/solution.py
@@ -65,7 +65,9 @@
     row_at = lax.axis_index("row")
     col_at = lax.axis_index("col")
     whole = gathered_copies(queries, "col", 2)
-    whole = lax.all_gather(whole, "row", axis=1, tiled=True)
+    whole = jnp.concatenate(
+        lax.all_to_all(jnp.stack([whole] * lax.axis_size("row")), "row", 0, 0), axis=1
+    )
     offset = (row_at * lax.axis_size("col") + col_at) * key_cache.shape[1]
     numer_part, peak_part, total_part = cache_partials(
         whole, key_cache, value_cache, lengths, offset

time: 747 us -> 822 us (1.10)
  waiting for transfers between devices: 404 us -> 462 us
    all_to_all x0 -> x1, waiting for transfers between devices: none -> 112 us  [body(): lax.all_to_all(jnp.stack([whole] * lax.axis_size('row')), 'row', 0, 0)]
    all_gather x1 -> x0, waiting for transfers between devices: 52.4 us -> none  [body(): whole = lax.all_gather(whole, 'row', axis=1, tiled=True)]
    while x17 -> x16, local copies, waits for them, and re-layouts: 38.3 us -> 25.7 us
    dynamic_slice x48 -> x56, local copies, waits for them, and re-layouts: 57.7 us -> 67.8 us  [cache_partials(): return lax.map(one_user, (whole, key_cache, value_cache, lengths))]
where the time goes in v1:
time: 822 us; the launch traced here: 819 us
  waiting for transfers between devices  462 us (56%)
  local copies, waits for them, and re-layouts  187 us (23%)
  matrix products  85.4 us (10%)
  other arithmetic  46.3 us (6%)
  blocking collectives  17.5 us (2%)
  between operations  13.6 us (2%)
    psum x1, waiting for transfers between devices, body(): numer, total = lax.psum((weighted, mass), ('row', 'col'))  211 us
    pmax x1, waiting for transfers between devices, body(): peak_all = lax.pmax(peak_part, ('row', 'col'))  138 us
    all_to_all x1, waiting for transfers between devices, body(): lax.all_to_all(jnp.stack([whole] * lax.axis_size('row')), 'row', 0, 0)  112 us
    dynamic_slice x56, local copies, waits for them, and re-layouts, cache_partials(): return lax.map(one_user, (whole, key_cache, value_cache, lengths))  67.8 us
    dot_general x8, matrix products, one_user(): jnp.einsum('kwgl,lkd->wkgd', weight.astype(jnp.bfloat16), v_heads, prefer...  57.4 us
    dynamic_update_slice x24, local copies, waits for them, and re-layouts, cache_partials(): return lax.map(one_user, (whole, key_cache, value_cache, lengths))  53.2 us
    mul x2, local copies, waits for them, and re-layouts, body(): numer_part.reshape(users, -1, HQ, HD) * factor[..., None]  26.6 us
    while x16, local copies, waits for them, and re-layouts  25.7 us
  transfers between devices with their start and end apart: 3, of which 3 were waited for; matrix products, arithmetic and copies ran while one was open for 0% of the time, Pallas kernels for 0%

profile of v1, /device:TPU:1, one launch (start us, length us, event | category | flops | bytes accessed | tf_op | source)
XLA Modules:
  0.0 819.5 jit_solution(5214636625929700745)
XLA Ops:
  7.6 17.5 %all_to_all.10 = bf16[8,8,8,512]{3,2,1,0:T(8,128)(2,1)S(1)} all-to-all(bf16[8,8,8,512]{3,2,1,0:T(8,128)(2,1)S(1)} %broadcast_in_dim.46), channel_id=1, replica_groups=mesh['row'=16,'col'=8] {'col'}, dimensions={0} | all-to-all | bytes 1048576 | tf_op jit(solution)/shard_map/all_to_all | solution.py:19
  25.2 4.3 stack.3
  29.4 7.5 all-to-all-start.1
  37.1 112.5 %all-to-all-done.1 = bf16[16,8,8,4096]{3,2,1,0:T(8,128)(2,1)} async-done(((bf16[16,8,8,4096]{3,2,1,0:T(8,128)(2,1)}), bf16[16,8,8,4096]{3,2,1,0:T(8,128)(2,1)}, u32[]{:S(2)}, u32[]{:S(2)}) %all-to-all-start.1) | async-done | bytes 8388640 | tf_op jit(solution)/shard_map/all_to_all | solution.py:69
  149.6 7.7 copy.60
  157.3 253.4 %while.14 = (s32[]{:T(128)}, f32[8,128,4096]{2,1,0:T(8,128)}, f32[8,128,32]{1,2,0:T(8,128)}, f32[8,128,32]{1,2,0:T(8,128)S(1)}, bf16[8,512,1024]{2,1,0:T(8,128)(...) while((s32[]{:T(128)}, f32[8,128,4096]{2,1,0:T(8,128)}, ...), condition=%wide.region_3.4_spmd, body=%wide.region_0.3_spmd.sunk | while | flops 1100997632 | bytes 85068960 | solution.py:58
  163.8 3.2 fusion.45
  167.0 3.2 copy-done.1
  175.7 7.2 fusion.46
  182.9 2.9 copy.68
  185.8 3.1 constant_dynamic-update-slice_fusion.2
  195.5 3.2 fusion.45
  198.6 3.2 copy-done.1
  207.4 7.2 fusion.46
  214.6 2.9 copy.68
  217.5 3.1 constant_dynamic-update-slice_fusion.2
  227.1 3.2 fusion.45
  230.3 3.2 copy-done.1
  239.1 7.2 fusion.46
  246.2 2.9 copy.68
  249.2 3.1 constant_dynamic-update-slice_fusion.2
  258.8 3.2 fusion.45
  261.9 3.2 copy-done.1
  270.7 7.2 fusion.46
  277.9 2.9 copy.68
  280.8 3.1 constant_dynamic-update-slice_fusion.2
  290.5 3.2 fusion.45
  293.6 3.2 copy-done.1
  302.4 7.2 fusion.46
  309.6 2.9 copy.68
  312.5 3.2 constant_dynamic-update-slice_fusion.2
  322.2 3.2 fusion.45
  325.3 3.2 copy-done.1
  334.1 7.2 fusion.46
  344.2 3.1 constant_dynamic-update-slice_fusion.2
  353.8 3.2 fusion.45
  357.0 3.2 copy-done.1
  365.8 7.2 fusion.46
  375.9 3.1 constant_dynamic-update-slice_fusion.2
  385.5 3.2 fusion.45
  388.7 3.2 copy-done.1
  397.5 7.2 fusion.46
  407.6 3.1 constant_dynamic-update-slice_fusion.2
  410.8 137.8 %all-reduce.4.cloned.1.call-done = f32[8,128,32]{1,2,0:T(8,128)} async-done(((f32[8,128,32]{1,2,0:T(8,128)}), f32[8,128,32]{1,2,0:T(8,128)}) %all-reduce.4.cloned.1.call-update) | async-done | bytes 131088 | tf_op jit(solution)/shard_map/pmax | solution.py:75
  550.4 8.4 %mul.66 = f32[8,128,32,128]{3,2,1,0:T(8,128)} broadcast(f32[8,128,32]{2,1,0:T(8,128)S(1)} %copy.45), dimensions={0,1,2} | broadcast | bytes 16908288 | tf_op jit(solution)/shard_map/mul | solution.py:77
  558.8 18.2 %mul.67 = f32[8,128,4096]{2,1,0:T(8,128)} reshape(f32[8,128,32,128]{3,2,1,0:T(8,128)} %mul.66) | data formatting | bytes 33554432 | tf_op jit(solution)/shard_map/mul | solution.py:77
  577.0 17.9 %mul.68 = f32[8,128,4096]{2,1,0:T(8,128)} multiply(f32[8,128,4096]{2,1,0:T(8,128)} %get-tuple-element.54, f32[8,128,4096]{2,1,0:T(8,128)} %mul.67) | non-fusion elementwise | flops 4194304 | bytes 50331648 | tf_op jit(solution)/shard_map/mul | solution.py:77
  598.4 211.3 %all-reduce.6.cloned.1.call-done = (f32[8,128,32]{1,2,0:T(8,128)}, f32[8,128,4096]{2,1,0:T(8,128)}) async-done(((f32[8,128,32]{1,2,0:T(8,128)}, f32[8,128,4096]{2,1,0:T(8,128)}), (f32[8,128,32]{1,2,0:T(8,128)}, f32[8,128,4096]{2,1,0:T(8,128)})) %all-reduce.6.cloned.1.call-update) | async-done | bytes 16908304 | tf_op jit(solution)/shard_map/psum | solution.py:88
  (117 shorter events, 114.6 us)
Async XLA Ops:
  6.5 588.4 %copy-start = (bf16[1024,1024]{1,0:T(8,128)(2,1)S(1)}, bf16[1024,1024]{1,0:T(8,128)(2,1)}, u32[]{:S(2)}) copy-start(bf16[1024,1024]{1,0:T(8,128)(2,1)} %param.12) | copy-start | bytes 6291460
  29.4 120.1 %all-to-all-start.1 = ((bf16[16,8,8,4096]{3,2,1,0:T(8,128)(2,1)}), bf16[16,8,8,4096]{3,2,1,0:T(8,128)(2,1)}, u32[]{:S(2)}, u32[]{:S(2)}) async-start(bf16[16,8,8,4096]{3,2,1,0:T(8,128)(2,1)} %stack.3), calls=%async_computation.1 | async-start | bytes 16777216 | tf_op jit(solution)/shard_map/all_to_all | solution.py:69
  37.0 511.6 %all-reduce.4.cloned.1.call-start = ((), (), s32[]{:S(2)}) async-start(), calls=%async_computation.2 | async-start | bytes 262144 | tf_op jit(solution)/shard_map/pmax | solution.py:75
  37.1 120.2 %copy-start.4 = (s32[8]{0:T(128)S(1)}, s32[8]{0:T(128)}, u32[]{:S(2)}) copy-start(s32[8]{0:T(128)} %param.14) | copy-start | bytes 100
  166.9 3.2 copy-start.1
  198.6 3.2 copy-start.1
  230.3 3.2 copy-start.1
  261.9 3.2 copy-start.1
  293.6 3.2 copy-start.1
  325.3 3.2 copy-start.1
  357.0 3.2 copy-start.1
  388.7 3.2 copy-start.1
  410.7 399.1 %all-reduce.6.cloned.1.call-start = ((), (), s32[]{:S(2)}) async-start(), calls=%async_computation.3 | async-start | bytes 33816576 | tf_op jit(solution)/shard_map/psum | solution.py:88
  594.9 0.7 copy-start.3
  594.9 1.3 copy-start.2
Sparse Core Ops, SparseCore 0:
  410.8 137.7 all-reduce.3
  595.0 214.6 all-reduce.5
